TPU v7x, 256 devices: a whole 4x4x8 slice. The times are simulated.
256 devices in a mesh: grp: 8 (over y, x_lo), ctx: 32 (over z, x_hi, core).
Axes of the slice: x: 4 (x_hi: 2, x_lo: 2; x = x_hi * 2 + x_lo), y: 4, z: 8, core: 2. Of those that a mesh axis runs over, the one named last changes fastest.
Arguments:
- tokens: bfloat16 [8, 2048, 4096], P('grp', 'ctx'), may hold values from -8 to 8
- req_lengths: int32 [8, 8], replicated, may hold values from 1 to 1088, 2048 in all within a row
- req_adapter: int32 [8, 8], replicated, may hold values from 0 to 7
- adapter_slot: int32 [8], replicated, may hold values from 0 to 7, each once
- query_weight: bfloat16 [4096, 4096], P(None, 'grp'), may hold values from -0.109375 to 0.109375
- key_weight: bfloat16 [4096, 1024], P(None, 'grp'), may hold values from -0.109375 to 0.109375
- value_weight: bfloat16 [4096, 1024], P(None, 'grp'), may hold values from -0.09375 to 0.09375
- w_out: bfloat16 [4096, 4096], P('grp'), may hold values from -0.09375 to 0.09375
- down_qkv: bfloat16 [8, 48, 4096], P('grp'), may hold values from -0.09375 to 0.09375
- up_query: bfloat16 [8, 16, 4096], P('grp'), may hold values from -0.59765625 to 0.59765625
- up_kv: bfloat16 [8, 2, 16, 1024], P('grp'), may hold values from -0.59765625 to 0.59765625
- down_out: bfloat16 [8, 16, 4096], P('grp'), may hold values from -0.09375 to 0.09375
- up_out: bfloat16 [8, 16, 4096], P('grp'), may hold values from -0.59765625 to 0.59765625
Outputs:
- mixed: bfloat16 [8, 2048, 4096], P('grp', 'ctx')
Inputs may be any that keep to these rules, and one draw needn't show every extreme that they name: `req_lengths`: row b holds the lengths of group b's 8 requests in order; each row sums to 2048 and its longest request has 1088 positions. adapter a's tables stand at slot adapter_slot[a]; every slot is used by one adapter.
All inputs are finite; a program needn't handle non-finite values.
Results may differ from a plain program's by a relative error of at most 0.015.
The roundings to bfloat16 on the way count: a program that leaves them out, or rounds other values in their place, can miss the bound.
Values may be sent and summed in bfloat16 or wider, within the bound.
A program may use at most 128 MiB of HBM per device.

v0:
```python
import math
import jax
import jax.numpy as jnp
from jax import lax
from jax.sharding import PartitionSpec as P

MODEL_WIDTH = 4096
HD = 128
ADAPTER_RANK = 16
ROPE_BASE = 500000.0
ADAPTER_SCALE = 2.0
MASKED_SCORE = -1e30


def request_info(lengths, adapter_ids, positions):
    req_ends = jnp.cumsum(lengths, axis=-1)
    starts = req_ends - lengths
    segment = jnp.sum((req_ends[..., None, :] <= positions[:, None]).astype(jnp.int32), axis=-1)
    req_picks = (segment[..., None] == jnp.arange(lengths.shape[-1], dtype=jnp.int32)).astype(
        jnp.int32
    )
    req_begin = jnp.sum(req_picks * starts[..., None, :], axis=-1)
    req_owner = jnp.sum(req_picks * adapter_ids[..., None, :], axis=-1)
    return (segment, req_begin, req_owner)


def rotate(values, offsets):
    half_width = values.shape[-1] // 2
    frequency = jnp.exp(
        jnp.arange(half_width, dtype=jnp.float32) * (-2.0 * math.log(ROPE_BASE) / values.shape[-1])
    )
    angles = offsets[..., None, None] * frequency
    cosine = jnp.cos(angles)
    sine = jnp.sin(angles)
    lower_half = values[..., :half_width]
    upper_half = values[..., half_width:]
    return jnp.concatenate(
        [lower_half * cosine - upper_half * sine, upper_half * cosine + lower_half * sine], axis=-1
    )


def widen_rows(adapter_middle, adapter_onehot, upward_table):
    masked_scores = adapter_onehot[:, :, None] * adapter_middle[:, None, :]
    flat_rows = masked_scores.reshape(
        masked_scores.shape[0], upward_table.shape[0] * upward_table.shape[1]
    )
    return jnp.dot(
        flat_rows,
        upward_table.reshape(upward_table.shape[0] * upward_table.shape[1], upward_table.shape[2]),
        preferred_element_type=jnp.float32,
    )


def narrow_rows(input_rows, down_table, adapter_onehot):
    every_term = jnp.einsum(
        "gtd,afd->gtaf", input_rows, down_table, preferred_element_type=jnp.float32
    )
    return jnp.sum(every_term * adapter_onehot[..., None].astype(jnp.float32), axis=2).astype(
        jnp.bfloat16
    )


def body(
    tokens,
    req_lengths,
    req_adapter,
    adapter_slot,
    query_weight,
    key_weight,
    value_weight,
    w_out,
    down_qkv,
    up_query,
    up_kv,
    down_out,
    up_out,
):
    groups = req_lengths.shape[0]
    token_matrix = tokens.shape[1]
    adapters = adapter_slot.shape[0]
    group_index = lax.axis_index("grp")
    block_index = lax.axis_index("ctx")
    q_cols = query_weight.shape[1]
    kv_cols = key_weight.shape[1]
    kv_local = kv_cols // HD
    heads_per_kv = q_cols // kv_cols
    positions = block_index * token_matrix + jnp.arange(token_matrix, dtype=jnp.int32)
    seg_rows, begin_rows, owner_rows = request_info(req_lengths, req_adapter, positions)
    onehot_rows = (owner_rows[..., None] == jnp.arange(adapters, dtype=jnp.int32)).astype(
        jnp.bfloat16
    )
    own_hot = lax.dynamic_slice_in_dim(onehot_rows, group_index, 1, 0)
    down_slots, upq_slots, upkv_slots, downo_slots, upo_slots = (
        lax.all_gather(down_qkv, "grp", axis=0, tiled=True),
        lax.all_gather(up_query, "grp", axis=0, tiled=True),
        lax.all_gather(up_kv, "grp", axis=0, tiled=True),
        lax.all_gather(down_out, "grp", axis=0, tiled=True),
        lax.all_gather(up_out, "grp", axis=0, tiled=True),
    )
    upq_slots = lax.dynamic_slice_in_dim(upq_slots, group_index * q_cols, q_cols, 2)
    upkv_slots = lax.dynamic_slice_in_dim(upkv_slots, group_index * kv_cols, kv_cols, 3)
    downo_slots = lax.dynamic_slice_in_dim(downo_slots, group_index * q_cols, q_cols, 2)
    down_adapter = jnp.take(down_slots, adapter_slot, axis=0)
    up_query_adapter = jnp.take(upq_slots, adapter_slot, axis=0)
    up_key_value_adapter = jnp.take(upkv_slots, adapter_slot, axis=0)
    downo_ad = jnp.take(downo_slots, adapter_slot, axis=0)
    up_output_adapter = jnp.take(upo_slots, adapter_slot, axis=0)
    all_requests = lax.all_gather(tokens, "grp", axis=0, tiled=True)
    adapter_middle = narrow_rows(all_requests, down_adapter, onehot_rows)
    count_of_rows = groups * token_matrix
    flat_inputs = all_requests.reshape(count_of_rows, MODEL_WIDTH)
    onehot_flat = onehot_rows.reshape(count_of_rows, adapters)
    middle_flat = adapter_middle.reshape(count_of_rows, 3 * ADAPTER_RANK)
    offsets = (positions[None, :] - begin_rows).astype(jnp.float32).reshape(count_of_rows)
    query_total = jnp.dot(
        flat_inputs, query_weight, preferred_element_type=jnp.float32
    ) + ADAPTER_SCALE * widen_rows(middle_flat[:, 0:ADAPTER_RANK], onehot_flat, up_query_adapter)
    key_total = jnp.dot(
        flat_inputs, key_weight, preferred_element_type=jnp.float32
    ) + ADAPTER_SCALE * widen_rows(
        middle_flat[:, ADAPTER_RANK : 2 * ADAPTER_RANK], onehot_flat, up_key_value_adapter[:, 0]
    )
    value_total = jnp.dot(
        flat_inputs, value_weight, preferred_element_type=jnp.float32
    ) + ADAPTER_SCALE * widen_rows(
        middle_flat[:, 2 * ADAPTER_RANK : 3 * ADAPTER_RANK], onehot_flat, up_key_value_adapter[:, 1]
    )
    query = rotate(query_total.reshape(count_of_rows, q_cols // HD, HD), offsets).astype(
        jnp.bfloat16
    )
    query = query.reshape(groups, token_matrix, kv_local, heads_per_kv, HD)
    key = (
        rotate(key_total.reshape(count_of_rows, kv_local, HD), offsets)
        .astype(jnp.bfloat16)
        .reshape(groups, token_matrix, kv_cols)
    )
    value = value_total.astype(jnp.bfloat16).reshape(groups, token_matrix, kv_cols)
    score_scale = math.sqrt(HD)
    start_top = jnp.full((groups, token_matrix, kv_local, heads_per_kv), MASKED_SCORE, jnp.float32)
    key_piece = lax.all_gather(key, "ctx", axis=1, tiled=True)
    value_piece = lax.all_gather(value, "ctx", axis=1, tiled=True)
    key_count = key_piece.shape[1]
    key_positions = jnp.arange(key_count, dtype=jnp.int32)
    key_segment, unused_begin, unused_owner = request_info(req_lengths, req_adapter, key_positions)
    allowed = (
        (key_segment[:, None, :] == seg_rows[:, :, None])
        & (key_positions[None, None, :] <= positions[None, :, None])
        & (key_positions[None, None, :] >= 0)
    )
    key_heads = key_piece.reshape(groups, key_count, kv_local, HD)
    value_heads = value_piece.reshape(groups, key_count, kv_local, HD)
    scores = (
        jnp.einsum("gtkjd,gskd->gtkjs", query, key_heads, preferred_element_type=jnp.float32)
        / score_scale
    )
    mask_full = allowed[:, :, None, None, :]
    scores = jnp.where(mask_full, scores, MASKED_SCORE)
    new_top = jnp.maximum(start_top, jnp.max(scores, axis=-1))
    weights = jnp.where(mask_full, jnp.exp(scores - new_top[..., None]), 0.0)
    new_sum = jnp.sum(weights, axis=-1)
    new_accum = jnp.einsum(
        "gtkjs,gskd->gtkjd",
        weights.astype(jnp.bfloat16),
        value_heads,
        preferred_element_type=jnp.float32,
    )
    final_state = (new_top, new_sum, new_accum)
    final_top, final_sum, final_accum = final_state
    attended = (
        (final_accum / final_sum[..., None])
        .astype(jnp.bfloat16)
        .reshape(groups, token_matrix, q_cols)
    )
    attended_flat = attended.reshape(count_of_rows, q_cols)
    mid_terms = jnp.einsum(
        "pc,arc->par", attended_flat, downo_ad, preferred_element_type=jnp.float32
    )
    out_terms = jnp.sum(mid_terms * onehot_flat[..., None].astype(jnp.float32), axis=1).reshape(
        groups, token_matrix, ADAPTER_RANK
    )
    output_middle = lax.psum_scatter(
        out_terms.astype(jnp.bfloat16), "grp", scatter_dimension=0, tiled=True
    )
    partial_term = jnp.einsum("gtc,cd->gtd", attended, w_out, preferred_element_type=jnp.float32)
    base_product = lax.psum_scatter(
        lax.optimization_barrier(partial_term.astype(jnp.bfloat16))
        .astype(jnp.float32)
        .astype(jnp.bfloat16),
        "grp",
        scatter_dimension=0,
        tiled=True,
    ).astype(jnp.float32)
    adapter_delta = widen_rows(
        output_middle.reshape(token_matrix, ADAPTER_RANK),
        own_hot.reshape(token_matrix, adapters),
        up_output_adapter,
    )
    return (
        base_product + ADAPTER_SCALE * adapter_delta.reshape(1, token_matrix, MODEL_WIDTH)
    ).astype(jnp.bfloat16)


def solution(mesh):
    placed = (
        P("grp", "ctx", None),
        P(),
        P(),
        P(),
        P(None, "grp"),
        P(None, "grp"),
        P(None, "grp"),
        P("grp", None),
        P("grp", None, None),
        P("grp", None, None),
        P("grp", None, None, None),
        P("grp", None, None),
        P("grp", None, None),
    )
    return jax.shard_map(
        body, mesh=mesh, in_specs=placed, out_specs=P("grp", "ctx", None), check_vma=False
    )
```

profile of v0, /device:TPU:1, one launch (start us, length us, event | category | flops | bytes accessed | tf_op | source)
XLA Modules:
  0.0 638.5 jit_solution(13202051979169333373)
XLA Ops:
  13.3 29.5 %all_gather.26 = bf16[8,2,16,1024]{3,2,1,0:T(8,128)(2,1)S(1)} all-gather(bf16[1,2,16,1024]{3,2,1,0:T(8,128)(2,1)} %param.25), channel_id=1, replica_groups=mesh['grp'=8,'ctx'=32] {'grp'}, dimensions={0}, use_global_device_ids=true | all-gather | bytes 589824 | tf_op jit(solution)/shard_map/all_gather | solution.py:96
  43.5 49.3 %all-gather.10.cloned.1.call-done = bf16[8,48,4096]{2,1,0:T(8,128)(2,1)} async-done(((bf16[1,48,4096]{2,1,0:T(8,128)(2,1)}), bf16[8,48,4096]{2,1,0:T(8,128)(2,1)}) %all-gather.10.cloned.1.call-update) | async-done | bytes 3145744 | tf_op jit(solution)/shard_map/all_gather | solution.py:94
  92.8 4.3 gather_fusion
  97.1 91.1 %all-gather.8.cloned.1.call-done = bf16[8,64,4096]{2,1,0:T(8,128)(2,1)} async-done(((bf16[1,64,4096]{2,1,0:T(8,128)(2,1)}), bf16[8,64,4096]{2,1,0:T(8,128)(2,1)}) %all-gather.8.cloned.1.call-update) | async-done | bytes 4194320 | tf_op jit(solution)/shard_map/all_gather | solution.py:108
  188.2 6.2 fusion.20
  194.7 3.5 fusion.88
  198.4 1.2 fusion.58
  200.5 3.5 fusion.87
  207.4 20.7 %all-gather.16.cloned.1.call-done = bf16[8,16,4096]{2,1,0:T(8,128)(2,1)} async-done(((bf16[1,16,4096]{2,1,0:T(8,128)(2,1)}), bf16[8,16,4096]{2,1,0:T(8,128)(2,1)}) %all-gather.16.cloned.1.call-update) | async-done | bytes 1048592 | tf_op jit(solution)/shard_map/all_gather | solution.py:95
  228.1 0.9 constant_dynamic-slice_fusion
  229.6 42.5 %all-gather.18.cloned.1.call-done = bf16[8,16,4096]{2,1,0:T(8,128)(2,1)} async-done(((bf16[1,16,4096]{2,1,0:T(8,128)(2,1)}), bf16[8,16,4096]{2,1,0:T(8,128)(2,1)}) %all-gather.18.cloned.1.call-update) | async-done | bytes 1048592 | tf_op jit(solution)/shard_map/all_gather | solution.py:97
  272.1 0.9 constant_dynamic-slice_fusion.2
  273.5 5.8 fusion.89
  281.4 84.8 %all-gather.14.cloned.1.call-done = bf16[8,2048,128]{2,1,0:T(8,128)(2,1)} async-done(((bf16[8,64,128]{2,1,0:T(8,128)(2,1)}), bf16[8,2048,128]{2,1,0:T(8,128)(2,1)}) %all-gather.14.cloned.1.call-update) | async-done | bytes 4194320 | tf_op jit(solution)/shard_map/all_gather | solution.py:140
  366.2 10.0 %fusion = (f32[8,64,4]{1,2,0:T(4,128)S(1)}, f32[8,2048,64,4]{1,2,3,0:T(8,128)}) fusion(pred[8,64,2048]{2,1,0:T(8,128)(4,1)S(1)} %compare_and_fusion, bf16[8,64,4,64]{3,1,2,0:T(8,128)(2,1)S(1)} %copy.52, bf16[8,64,4,64]{3,1,2,0:T(8,128)(2,1)S(1)} %copy.51, bf16[8,2048,128]{2,1,0:T(8,128)(2,1)} %all-gather.14.cloned.1.call-done), kind=kOutput, calls=%fused_computation.7 | convolution fusion | flops 1087371264 | bytes 22552576 | tf_op jit(solution)/shard_map/gtkjd,gskd->gtkjs/dot_general | solution.py:153
  376.2 8.7 %fusion.1 = f32[8,64,4]{1,2,0:T(4,128)S(1)} fusion(f32[8,2048,64,4]{1,2,3,0:T(8,128)} %get-tuple-element.26, f32[8,64,4]{1,2,0:T(4,128)S(1)} %broadcast_maximum_fusion, pred[8,64,2048]{2,1,0:T(8,128)(4,1)S(1)} %compare_and_fusion), kind=kLoop, calls=%fused_computation.8 | loop fusion | flops 20969472 | bytes 17842176 | tf_op jit(solution)/shard_map/reduce_sum | solution.py:160
  384.8 67.4 %all-gather.12.cloned.1.call-done = bf16[8,2048,128]{2,1,0:T(8,128)(2,1)} async-done(((bf16[8,64,128]{2,1,0:T(8,128)(2,1)}), bf16[8,2048,128]{2,1,0:T(8,128)(2,1)}) %all-gather.12.cloned.1.call-update) | async-done | bytes 4194320 | tf_op jit(solution)/shard_map/all_gather | solution.py:141
  452.2 9.8 %fusion.44 = bf16[8,64,1,4,128]{4,1,3,0,2:T(8,128)(2,1)S(1)} fusion(f32[8,2048,64,4]{1,2,3,0:T(8,128)} %get-tuple-element.26, f32[8,64,4]{1,2,0:T(4,128)S(1)} %broadcast_maximum_fusion, pred[8,64,2048]{2,1,0:T(8,128)(4,1)S(1)} %compare_and_fusion, bf16[8,2048,128]{2,1,0:T(8,128)(2,1)} %all-gather.12.cloned.1.call-done, f32[8,64,4]{1,2,0:T(4,128)S(1)} %fusion.1), kind=kOutput, calls=%fused_computation.47 | convolution fusion | flops 1095237632 | bytes 22560768 | tf_op jit(solution)/shard_map/gtkjs,gskd->gtkjd/dot_general | solution.py:161
  463.9 6.5 %convolution_convert_fusion = bf16[8,64,4096]{2,1,0:T(8,128)(2,1)} fusion(bf16[8,64,512]{2,1,0:T(8,128)(2,1)S(1)} %reshape.328, bf16[512,4096]{1,0:T(8,128)(2,1)} %param.22), kind=kOutput, calls=%fused_computation.13 | convolution fusion | flops 2149580800 | bytes 8912896 | tf_op jit(solution)/shard_map/gtc,cd->gtd/dot_general | solution.py:184
  470.4 18.1 %all-gather.20.cloned.1.call-done = bf16[8,16,4096]{2,1,0:T(8,128)(2,1)} async-done(((bf16[1,16,4096]{2,1,0:T(8,128)(2,1)}), bf16[8,16,4096]{2,1,0:T(8,128)(2,1)}) %all-gather.20.cloned.1.call-update) | async-done | bytes 1048592 | tf_op jit(solution)/shard_map/all_gather | solution.py:98
  488.6 1.8 gather_fusion.2
  490.4 39.1 %reduce-scatter.5.cloned.1.call-done = bf16[1,64,16]{1,2,0:T(8,128)(2,1)} async-done(((bf16[8,64,16]{1,2,0:T(8,128)(2,1)}), bf16[1,64,16]{1,2,0:T(8,128)(2,1)}) %reduce-scatter.5.cloned.1.call-update) | async-done | bytes 2064 | tf_op jit(solution)/shard_map/reduce_scatter | solution.py:181
  529.5 100.3 %reduce-scatter.3.cloned.1.call-done = bf16[1,64,4096]{2,1,0:T(8,128)(2,1)} async-done(((bf16[8,64,4096]{2,1,0:T(8,128)(2,1)}), bf16[1,64,4096]{2,1,0:T(8,128)(2,1)}) %reduce-scatter.3.cloned.1.call-update) | async-done | bytes 524304 | tf_op jit(solution)/shard_map/reduce_scatter | solution.py:185
  629.8 2.2 fusion.10
  (70 shorter events, 16.9 us)
Async XLA Ops:
  6.5 188.2 %copy-start = (bf16[4096,128]{1,0:T(8,128)(2,1)S(1)}, bf16[4096,128]{1,0:T(8,128)(2,1)}, u32[]{:S(2)}) copy-start(bf16[4096,128]{1,0:T(8,128)(2,1)} %param.20) | copy-start | bytes 3145732
  6.5 86.3 %all-gather.10.cloned.1.call-start = ((), (), s32[]{:S(2)}) async-start(), calls=%async_computation.3 | async-start | bytes 3538944 | tf_op jit(solution)/shard_map/all_gather | solution.py:94
  7.3 181.0 %all-gather.8.cloned.1.call-start = ((), (), s32[]{:S(2)}) async-start(), calls=%async_computation.2 | async-start | bytes 4718592 | tf_op jit(solution)/shard_map/all_gather | solution.py:108
  8.0 220.1 %all-gather.16.cloned.1.call-start = ((), (), s32[]{:S(2)}) async-start(), calls=%async_computation.6 | async-start | bytes 1179648 | tf_op jit(solution)/shard_map/all_gather | solution.py:95
  8.7 263.3 %all-gather.18.cloned.1.call-start = ((), (), s32[]{:S(2)}) async-start(), calls=%async_computation.8 | async-start | bytes 1179648 | tf_op jit(solution)/shard_map/all_gather | solution.py:97
  9.3 356.9 %all-gather.14.cloned.1.call-start = ((), (), s32[]{:S(2)}) async-start(), calls=%async_computation.5 | async-start | bytes 4325376 | tf_op jit(solution)/shard_map/all_gather | solution.py:140
  194.5 6.0 copy-start.2
  200.5 251.8 %all-gather.12.cloned.1.call-start = ((), (), s32[]{:S(2)}) async-start(), calls=%async_computation.4 | async-start | bytes 4325376 | tf_op jit(solution)/shard_map/all_gather | solution.py:141
  204.9 283.7 %all-gather.20.cloned.1.call-start = ((), (), s32[]{:S(2)}) async-start(), calls=%async_computation.10 | async-start | bytes 1179648 | tf_op jit(solution)/shard_map/all_gather | solution.py:98
  205.6 323.9 %reduce-scatter.5.cloned.1.call-start = ((), (), s32[]{:S(2)}) async-start(), calls=%async_computation.9 | async-start | bytes 36864 | tf_op jit(solution)/shard_map/reduce_scatter | solution.py:181
  463.9 165.9 %reduce-scatter.3.cloned.1.call-start = ((), (), s32[]{:S(2)}) async-start(), calls=%async_computation.7 | async-start | bytes 4718592 | tf_op jit(solution)/shard_map/reduce_scatter | solution.py:185
  470.4 161.6 %copy-start.1 = (bf16[4096,128]{1,0:T(8,128)(2,1)S(1)}, bf16[4096,128]{1,0:T(8,128)(2,1)}, u32[]{:S(2)}) copy-start(bf16[4096,128]{1,0:T(8,128)(2,1)} %param.20) | copy-start | bytes 3145732
Sparse Core Ops, SparseCore 0:
  9.1 83.6 all-gather.9
  94.6 93.5 all-gather.7
  190.0 38.0 all-gather.15
  229.8 42.2 all-gather.17
  274.7 91.4 all-gather.13
  368.9 83.2 all-gather.11
  454.0 34.5 all-gather.19
  491.1 38.3 reduce-scatter.4
  532.1 97.6 reduce-scatter.2
where the time goes:
time: 639 us
  waiting for transfers between devices  517 us (81%)
  matrix products  49.3 us (8%)
  blocking collectives  29.5 us (5%)
  other arithmetic  16.3 us (3%)
  between operations  13.5 us (2%)
  local copies, waits for them, and re-layouts  13 us (2%)
    reduce_scatter x1, waiting for transfers between devices, body(): lax.psum_scatter(lax.optimization_barrier(partial_term.astype(jnp.bfloat1...  100 us
    all_gather x1, waiting for transfers between devices, body(): all_requests = lax.all_gather(tokens, 'grp', axis=0, tiled=True)  91.1 us
    all_gather x1, waiting for transfers between devices, body(): key_piece = lax.all_gather(key, 'ctx', axis=1, tiled=True)  84.8 us
    all_gather x1, waiting for transfers between devices, body(): value_piece = lax.all_gather(value, 'ctx', axis=1, tiled=True)  67.4 us
    all_gather x1, waiting for transfers between devices, body(): lax.all_gather(down_qkv, 'grp', axis=0, tiled=True)  49.3 us
    all_gather x1, waiting for transfers between devices, body(): lax.all_gather(down_out, 'grp', axis=0, tiled=True)  42.5 us
    reduce_scatter x1, waiting for transfers between devices, body(): lax.psum_scatter(out_terms.astype(jnp.bfloat16), 'grp', scatter_dimension...  39.1 us
    all_gather x1, blocking collectives, body(): lax.all_gather(up_kv, 'grp', axis=0, tiled=True)  29.5 us
  transfers between devices with their start and end apart: 9, of which 9 were waited for; matrix products, arithmetic and copies ran while one was open for 12% of the time, Pallas kernels for 0%

commit v1 on v0

--- a/solution.py
+++ b/solution.py
@@ -1,3 +1,4 @@
+import functools
 import math
 import jax
 import jax.numpy as jnp
@@ -10,6 +11,18 @@
 ROPE_BASE = 500000.0
 ADAPTER_SCALE = 2.0
 MASKED_SCORE = -1e30
+
+
+def check_tables(u_in, which_axis):
+    return jnp.concatenate(
+        lax.all_to_all(
+            jnp.stack([u_in for _ in range(lax.axis_size(which_axis))], 0), which_axis, 0, 0
+        ),
+        0,
+    )
+
+
+create_pages_on_mesh = functools.partial(check_tables, which_axis="grp")
 
 
 def request_info(lengths, adapter_ids, positions):
@@ -94,7 +107,7 @@
         lax.all_gather(down_qkv, "grp", axis=0, tiled=True),
         lax.all_gather(up_query, "grp", axis=0, tiled=True),
         lax.all_gather(up_kv, "grp", axis=0, tiled=True),
-        lax.all_gather(down_out, "grp", axis=0, tiled=True),
+        create_pages_on_mesh(down_out),
         lax.all_gather(up_out, "grp", axis=0, tiled=True),
     )
     upq_slots = lax.dynamic_slice_in_dim(upq_slots, group_index * q_cols, q_cols, 2)

time: 639 us -> 601 us (0.941)
  waiting for transfers between devices: 517 us -> 475 us
    all_gather x1 -> x0, waiting for transfers between devices: 42.5 us -> none  [body(): lax.all_gather(down_out, 'grp', axis=0, tiled=True)]
    all_to_all x0 -> x1, waiting for transfers between devices: none -> 24.4 us  [check_tables(): lax.all_to_all(jnp.stack([u_in for _ in range(lax.axis_size(which_axis))]...]
    all_gather x1, waiting for transfers between devices: 20.7 us -> 0.17 us  [body(): lax.all_gather(up_query, 'grp', axis=0, tiled=True)]
  transfers between devices with their start and end apart: 9 -> 9, of which waited for: 9 -> 9; matrix products, arithmetic and copies ran while one was open for 12% -> 13% of each run, Pallas kernels for 0% -> 0%
where the time goes in v1:
time: 601 us
  waiting for transfers between devices  475 us (79%)
  matrix products  49.3 us (8%)
  blocking collectives  28.9 us (5%)
  other arithmetic  16.3 us (3%)
  between operations  13.8 us (2%)
  local copies, waits for them, and re-layouts  13.2 us (2%)
    reduce_scatter x1, waiting for transfers between devices, body(): lax.psum_scatter(lax.optimization_barrier(partial_term.astype(jnp.bfloat1...  100 us
    all_gather x1, waiting for transfers between devices, body(): all_requests = lax.all_gather(tokens, 'grp', axis=0, tiled=True)  90.5 us
    all_gather x1, waiting for transfers between devices, body(): key_piece = lax.all_gather(key, 'ctx', axis=1, tiled=True)  82.3 us
    all_gather x1, waiting for transfers between devices, body(): value_piece = lax.all_gather(value, 'ctx', axis=1, tiled=True)  67.4 us
    all_gather x1, waiting for transfers between devices, body(): lax.all_gather(down_qkv, 'grp', axis=0, tiled=True)  50.4 us
    reduce_scatter x1, waiting for transfers between devices, body(): lax.psum_scatter(out_terms.astype(jnp.bfloat16), 'grp', scatter_dimension...  39.3 us
    all_gather x1, blocking collectives, body(): lax.all_gather(up_kv, 'grp', axis=0, tiled=True)  28.9 us
    all_to_all x1, waiting for transfers between devices, check_tables(): lax.all_to_all(jnp.stack([u_in for _ in range(lax.axis_size(which_axis))]...  24.4 us
  transfers between devices with their start and end apart: 9, of which 9 were waited for; matrix products, arithmetic and copies ran while one was open for 13% of the time, Pallas kernels for 0%

profile of v1, /device:TPU:1, one launch (start us, length us, event | category | flops | bytes accessed | tf_op | source)
XLA Modules:
  0.0 600.6 jit_solution(6344678096145553087)
XLA Ops:
  12.7 28.9 %all_gather.23 = bf16[8,2,16,1024]{3,2,1,0:T(8,128)(2,1)S(1)} all-gather(bf16[1,2,16,1024]{3,2,1,0:T(8,128)(2,1)} %param.25), channel_id=1, replica_groups=mesh['grp'=8,'ctx'=32] {'grp'}, dimensions={0}, use_global_device_ids=true | all-gather | bytes 589824 | tf_op jit(solution)/shard_map/all_gather | solution.py:109
  42.4 50.4 %all-gather.9.cloned.1.call-done = bf16[8,48,4096]{2,1,0:T(8,128)(2,1)} async-done(((bf16[1,48,4096]{2,1,0:T(8,128)(2,1)}), bf16[8,48,4096]{2,1,0:T(8,128)(2,1)}) %all-gather.9.cloned.1.call-update) | async-done | bytes 3145744 | tf_op jit(solution)/shard_map/all_gather | solution.py:107
  92.8 4.3 gather_fusion
  97.1 90.5 %all-gather.7.cloned.1.call-done = bf16[8,64,4096]{2,1,0:T(8,128)(2,1)} async-done(((bf16[1,64,4096]{2,1,0:T(8,128)(2,1)}), bf16[8,64,4096]{2,1,0:T(8,128)(2,1)}) %all-gather.7.cloned.1.call-update) | async-done | bytes 4194320 | tf_op jit(solution)/shard_map/all_gather | solution.py:121
  187.6 6.2 %fusion.20 = bf16[8,64,48]{1,2,0:T(8,128)(2,1)S(1)} fusion(bf16[8,64,4096]{2,1,0:T(8,128)(2,1)} %all-gather.7.cloned.1.call-done, bf16[8,48,4096]{2,1,0:T(8,128)(2,1)} %gather_fusion, pred[8]{0:T(512)(128)(4,1)S(1)} %compare_and_fusion.1, f32[8,64,8]{1,0,2:T(8,128)S(1)} %copy.47), kind=kOutput, calls=%fused_computation.30 | convolution fusion | flops 1612554240 | bytes 7405576 | tf_op jit(solution)/shard_map/gtd,afd->gtaf/dot_general | solution.py:68
  194.1 3.5 fusion.88
  197.9 1.2 fusion.58
  200.0 3.5 fusion.87
  204.3 1.1 stack.2
  205.4 3.8 all-to-all-start
  211.5 24.4 %all-to-all-done = bf16[8,1,16,4096]{3,2,1,0:T(8,128)(2,1)S(1)} async-done(((bf16[8,1,16,4096]{3,2,1,0:T(8,128)(2,1)}), bf16[8,1,16,4096]{3,2,1,0:T(8,128)(2,1)S(1)}, u32[]{:S(2)}, u32[]{:S(2)}) %all-to-all-start) | async-done | bytes 1048608 | tf_op jit(solution)/shard_map/all_to_all | solution.py:18
  236.7 0.9 constant_dynamic-slice_fusion
  238.2 5.8 fusion.89
  246.1 82.3 %all-gather.13.cloned.1.call-done = bf16[8,2048,128]{2,1,0:T(8,128)(2,1)} async-done(((bf16[8,64,128]{2,1,0:T(8,128)(2,1)}), bf16[8,2048,128]{2,1,0:T(8,128)(2,1)}) %all-gather.13.cloned.1.call-update) | async-done | bytes 4194320 | tf_op jit(solution)/shard_map/all_gather | solution.py:153
  328.3 10.0 %fusion = (f32[8,64,4]{1,2,0:T(4,128)S(1)}, f32[8,2048,64,4]{1,2,3,0:T(8,128)}) fusion(pred[8,64,2048]{2,1,0:T(8,128)(4,1)S(1)} %compare_and_fusion, bf16[8,64,4,64]{3,1,2,0:T(8,128)(2,1)S(1)} %copy.52, bf16[8,64,4,64]{3,1,2,0:T(8,128)(2,1)S(1)} %copy.51, bf16[8,2048,128]{2,1,0:T(8,128)(2,1)} %all-gather.13.cloned.1.call-done), kind=kOutput, calls=%fused_computation.7 | convolution fusion | flops 1087371264 | bytes 22552576 | tf_op jit(solution)/shard_map/gtkjd,gskd->gtkjs/dot_general | solution.py:166
  338.3 8.7 %fusion.1 = f32[8,64,4]{1,2,0:T(4,128)S(1)} fusion(f32[8,2048,64,4]{1,2,3,0:T(8,128)} %get-tuple-element.26, f32[8,64,4]{1,2,0:T(4,128)S(1)} %broadcast_maximum_fusion, pred[8,64,2048]{2,1,0:T(8,128)(4,1)S(1)} %compare_and_fusion), kind=kLoop, calls=%fused_computation.8 | loop fusion | flops 20969472 | bytes 17842176 | tf_op jit(solution)/shard_map/reduce_sum | solution.py:173
  347.0 67.4 %all-gather.11.cloned.1.call-done = bf16[8,2048,128]{2,1,0:T(8,128)(2,1)} async-done(((bf16[8,64,128]{2,1,0:T(8,128)(2,1)}), bf16[8,2048,128]{2,1,0:T(8,128)(2,1)}) %all-gather.11.cloned.1.call-update) | async-done | bytes 4194320 | tf_op jit(solution)/shard_map/all_gather | solution.py:154
  414.3 9.8 %fusion.44 = bf16[8,64,1,4,128]{4,1,3,0,2:T(8,128)(2,1)S(1)} fusion(f32[8,2048,64,4]{1,2,3,0:T(8,128)} %get-tuple-element.26, f32[8,64,4]{1,2,0:T(4,128)S(1)} %broadcast_maximum_fusion, pred[8,64,2048]{2,1,0:T(8,128)(4,1)S(1)} %compare_and_fusion, bf16[8,2048,128]{2,1,0:T(8,128)(2,1)} %all-gather.11.cloned.1.call-done, f32[8,64,4]{1,2,0:T(4,128)S(1)} %fusion.1), kind=kOutput, calls=%fused_computation.47 | convolution fusion | flops 1095237632 | bytes 22560768 | tf_op jit(solution)/shard_map/gtkjs,gskd->gtkjd/dot_general | solution.py:174
  426.0 6.5 %convolution_convert_fusion = bf16[8,64,4096]{2,1,0:T(8,128)(2,1)} fusion(bf16[8,64,512]{2,1,0:T(8,128)(2,1)S(1)} %reshape.333, bf16[512,4096]{1,0:T(8,128)(2,1)} %param.22), kind=kOutput, calls=%fused_computation.13 | convolution fusion | flops 2149580800 | bytes 8912896 | tf_op jit(solution)/shard_map/gtc,cd->gtd/dot_general | solution.py:197
  432.6 17.6 %all-gather.17.cloned.1.call-done = bf16[8,16,4096]{2,1,0:T(8,128)(2,1)} async-done(((bf16[1,16,4096]{2,1,0:T(8,128)(2,1)}), bf16[8,16,4096]{2,1,0:T(8,128)(2,1)}) %all-gather.17.cloned.1.call-update) | async-done | bytes 1048592 | tf_op jit(solution)/shard_map/all_gather | solution.py:111
  450.2 1.8 gather_fusion.2
  452.0 39.3 %reduce-scatter.5.cloned.1.call-done = bf16[1,64,16]{1,2,0:T(8,128)(2,1)} async-done(((bf16[8,64,16]{1,2,0:T(8,128)(2,1)}), bf16[1,64,16]{1,2,0:T(8,128)(2,1)}) %reduce-scatter.5.cloned.1.call-update) | async-done | bytes 2064 | tf_op jit(solution)/shard_map/reduce_scatter | solution.py:194
  491.3 100.2 %reduce-scatter.3.cloned.1.call-done = bf16[1,64,4096]{2,1,0:T(8,128)(2,1)} async-done(((bf16[8,64,4096]{2,1,0:T(8,128)(2,1)}), bf16[1,64,4096]{2,1,0:T(8,128)(2,1)}) %reduce-scatter.3.cloned.1.call-update) | async-done | bytes 524304 | tf_op jit(solution)/shard_map/reduce_scatter | solution.py:198
  591.5 2.2 fusion.10
  (72 shorter events, 16.4 us)
Async XLA Ops:
  6.5 187.6 %copy-start = (bf16[4096,128]{1,0:T(8,128)(2,1)S(1)}, bf16[4096,128]{1,0:T(8,128)(2,1)}, u32[]{:S(2)}) copy-start(bf16[4096,128]{1,0:T(8,128)(2,1)} %param.20) | copy-start | bytes 3145732
  6.5 86.3 %all-gather.9.cloned.1.call-start = ((), (), s32[]{:S(2)}) async-start(), calls=%async_computation.4 | async-start | bytes 3538944 | tf_op jit(solution)/shard_map/all_gather | solution.py:107
  7.3 180.4 %all-gather.7.cloned.1.call-start = ((), (), s32[]{:S(2)}) async-start(), calls=%async_computation.3 | async-start | bytes 4718592 | tf_op jit(solution)/shard_map/all_gather | solution.py:121
  8.0 228.7 %all-gather.15.cloned.1.call-start = ((), (), s32[]{:S(2)}) async-start(), calls=%async_computation.7 | async-start | bytes 1179648 | tf_op jit(solution)/shard_map/all_gather | solution.py:108
  8.7 319.6 %all-gather.13.cloned.1.call-start = ((), (), s32[]{:S(2)}) async-start(), calls=%async_computation.6 | async-start | bytes 4325376 | tf_op jit(solution)/shard_map/all_gather | solution.py:153
  193.9 6.1 %copy-start.2 = (bf16[4096,128]{1,0:T(8,128)(2,1)S(1)}, bf16[4096,128]{1,0:T(8,128)(2,1)}, u32[]{:S(2)}) copy-start(bf16[4096,128]{1,0:T(8,128)(2,1)} %param.21) | copy-start | bytes 3145732
  197.6 6.7 %copy-start.3 = (bf16[1,16,4096]{2,1,0:T(8,128)(2,1)S(1)}, bf16[1,16,4096]{2,1,0:T(8,128)(2,1)}, u32[]{:S(2)}) copy-start(bf16[1,16,4096]{2,1,0:T(8,128)(2,1)} %param.26) | copy-start | bytes 393220
  199.9 214.4 %all-gather.11.cloned.1.call-start = ((), (), s32[]{:S(2)}) async-start(), calls=%async_computation.5 | async-start | bytes 4325376 | tf_op jit(solution)/shard_map/all_gather | solution.py:154
  205.4 30.5 %all-to-all-start = ((bf16[8,1,16,4096]{3,2,1,0:T(8,128)(2,1)}), bf16[8,1,16,4096]{3,2,1,0:T(8,128)(2,1)S(1)}, u32[]{:S(2)}, u32[]{:S(2)}) async-start(bf16[8,1,16,4096]{3,2,1,0:T(8,128)(2,1)} %stack.2), calls=%async_computation.1 | async-start | bytes 2097152 | tf_op jit(solution)/shard_map/all_to_all | solution.py:18
  209.2 240.9 %all-gather.17.cloned.1.call-start = ((), (), s32[]{:S(2)}) async-start(), calls=%async_computation.10 | async-start | bytes 1179648 | tf_op jit(solution)/shard_map/all_gather | solution.py:111
  209.8 281.6 %reduce-scatter.5.cloned.1.call-start = ((), (), s32[]{:S(2)}) async-start(), calls=%async_computation.9 | async-start | bytes 36864 | tf_op jit(solution)/shard_map/reduce_scatter | solution.py:194
  426.0 165.5 %reduce-scatter.3.cloned.1.call-start = ((), (), s32[]{:S(2)}) async-start(), calls=%async_computation.8 | async-start | bytes 4718592 | tf_op jit(solution)/shard_map/reduce_scatter | solution.py:198
  432.5 161.2 %copy-start.1 = (bf16[4096,128]{1,0:T(8,128)(2,1)S(1)}, bf16[4096,128]{1,0:T(8,128)(2,1)}, u32[]{:S(2)}) copy-start(bf16[4096,128]{1,0:T(8,128)(2,1)} %param.20) | copy-start | bytes 3145732
Sparse Core Ops, SparseCore 0:
  9.1 83.6 all-gather.8
  94.6 93.0 all-gather.6
  189.4 47.2 all-gather.14
  239.4 88.8 all-gather.12
  331.0 83.2 all-gather.10
  416.0 34.1 all-gather.16
  452.6 38.6 reduce-scatter.4
  493.9 97.6 reduce-scatter.2
